TPU v7x, 128 devices: a whole 4x4x4 slice. The times are simulated.
128 devices in a mesh: req: 32 (over z, x, core), tp: 4 (over y).
Axes of the slice: x: 4, y: 4, z: 4, core: 2. Of those that a mesh axis runs over, the one named last changes fastest.
Arguments:
- tokens: bfloat16 [16384, 2560], P('req'), may hold values from -6 to 6
- lengths: int32 [32], P('req'), may hold values from 1 to 512, as said below
- page_slot: int32 [128], replicated, may hold values from 0 to 127, as said below
- trainer_layout: int32 [128], replicated, may hold values from 0 to 127, each once
- trainer_qkv: float32 [2560, 3840], P(('req', 'tp'))
- trainer_gateup: float32 [2560, 13824], P(('req', 'tp')), may hold values from -0.125 to 0.125
- attn_gain: float32 [2560], replicated, may hold values from 0.1 to 1.9
- ffn_gain: float32 [2560], replicated, may hold values from 0.1 to 1.9
- out_proj: bfloat16 [2560, 2560], P('tp'), may hold values from -0.125 to 0.125
- down_proj: bfloat16 [6912, 2560], P('tp'), may hold values from -0.078125 to 0.078125
Outputs:
- layer_out: bfloat16 [16384, 2560], P(('req', 'tp'))
- kv_cache: bfloat16 [128, 128, 1280], P('req', None, 'tp')
Inputs may be any that keep to these rules, and one draw needn't show every extreme that they name: `lengths`: heavy-tailed; some request has exactly 512. `page_slot`: a permutation; pool slot s belongs to request device s // 4; the 4 pages of one request belong to 4 different devices. `trainer_layout`: a permutation; shard s is the trainer shard on the device with index s over req and tp together.
All inputs are finite; a program needn't handle non-finite values.
Results may differ from a plain program's by a relative error of at most 0.0065.
The roundings to bfloat16 on the way count: a program that leaves them out, or rounds other values in their place, can miss the bound.
Values may be sent and summed in bfloat16 or wider, within the bound.
A program may use at most 192 MiB of HBM per device.

v0:
```python
import jax
import jax.numpy as jnp
from jax import lax
from jax.sharding import PartitionSpec as P

HD = 80
PAGE = 128
eps_norm = 1e-05
theta_base = 10000.0


def normed(values, gain):
    scale = lax.rsqrt(jnp.mean(values * values, axis=-1, keepdims=True) + eps_norm)
    return (values * scale * gain).astype(jnp.bfloat16)


def rotary(field, head_dim):
    half = head_dim // 2
    count = field.shape[0]
    freq = theta_base ** (-jnp.arange(half, dtype=jnp.float32) * 2.0 / head_dim)
    angles = jnp.arange(count, dtype=jnp.float32)[:, None] * freq[None, :]
    cosine = jnp.cos(angles)[:, None, :]
    sine = jnp.sin(angles)[:, None, :]
    first = field[..., :half]
    second = field[..., half:]
    return jnp.concatenate(
        [first * cosine - second * sine, second * cosine + first * sine], axis=-1
    )


def body(
    tokens,
    lengths,
    page_slot,
    trainer_layout,
    trainer_qkv,
    trainer_gateup,
    attn_gain,
    ffn_gain,
    out_proj,
    down_proj,
):
    n_tp = lax.axis_size("tp")
    n_req = lax.axis_size("req")
    devices = n_tp * n_req
    rows_each = trainer_qkv.shape[0]
    seq_len = tokens.shape[0]
    model_dim = tokens.shape[1]
    head_dim = HD
    local_heads = out_proj.shape[0] // head_dim
    group_cols = trainer_qkv.shape[1] // n_tp
    local_kv = (group_cols // head_dim - local_heads) // 2
    group = local_heads // local_kv
    q_cols = local_heads * head_dim
    k_cols = local_kv * head_dim
    ff_local = down_proj.shape[0]
    qkv_half, gu_half = (
        lax.all_to_all(
            trainer_qkv.astype(jnp.bfloat16), "tp", split_axis=1, concat_axis=0, tiled=True
        ),
        lax.all_to_all(
            trainer_gateup.astype(jnp.bfloat16), "tp", split_axis=1, concat_axis=0, tiled=True
        ),
    )
    x_f = tokens.astype(jnp.float32)
    x_norm = normed(x_f, attn_gain)
    inverse = (
        jnp.zeros((devices,), jnp.int32)
        .at[trainer_layout]
        .set(jnp.arange(devices, dtype=jnp.int32))
    )
    qkv_all, gu_all = (
        lax.all_gather(qkv_half, "req", axis=0, tiled=True),
        lax.all_gather(gu_half, "req", axis=0, tiled=True),
    )
    qkv_weight = qkv_all.reshape(devices, rows_each, qkv_all.shape[1])[inverse].reshape(
        model_dim, qkv_all.shape[1]
    )
    gu_weight = gu_all.reshape(devices, rows_each, gu_all.shape[1])[inverse].reshape(
        model_dim, gu_all.shape[1]
    )
    joined = jnp.dot(x_norm, qkv_weight, preferred_element_type=jnp.float32)
    query = rotary(joined[:, :q_cols].reshape(seq_len, local_heads, head_dim), head_dim)
    keys = rotary(
        joined[:, q_cols : q_cols + k_cols].reshape(seq_len, local_kv, head_dim), head_dim
    )
    query16 = query.astype(jnp.bfloat16).reshape(seq_len, local_kv, group, head_dim)
    keys16 = keys.astype(jnp.bfloat16)
    values16 = (
        joined[:, q_cols + k_cols :].reshape(seq_len, local_kv, head_dim).astype(jnp.bfloat16)
    )
    scores = jnp.einsum(
        "qkgd,skd->kgqs", query16, keys16, preferred_element_type=jnp.float32
    ) * head_dim ** (-0.5)
    slots = jnp.arange(seq_len, dtype=jnp.int32)
    length = lengths[0]
    allowed = (slots[None, :] <= slots[:, None]) & (slots[None, :] < length)
    scores = jnp.where(allowed[None, None], scores, -1e30)
    probs = jax.nn.softmax(scores, axis=-1).astype(jnp.bfloat16)
    context = jnp.einsum(
        "kgqs,skd->qkgd", probs, values16, preferred_element_type=jnp.float32
    ).astype(jnp.bfloat16)
    partial_out = jnp.dot(
        context.reshape(seq_len, q_cols), out_proj, preferred_element_type=jnp.float32
    )
    share = seq_len // n_tp
    tp_index = lax.axis_index("tp")
    mixed = lax.psum(partial_out, "tp")
    resid = x_f + mixed
    h_norm = normed(resid, ffn_gain)
    resid_share = lax.dynamic_slice_in_dim(resid, tp_index * share, share, 0)
    projected = jnp.dot(h_norm, gu_weight, preferred_element_type=jnp.float32)
    hidden = (jax.nn.silu(projected[:, :ff_local]) * projected[:, ff_local:]).astype(jnp.bfloat16)
    down = jnp.dot(hidden, down_proj, preferred_element_type=jnp.float32)
    added = lax.psum_scatter(down, "tp", scatter_dimension=0, tiled=True)
    share_slots = tp_index * share + jnp.arange(share, dtype=jnp.int32)
    live_share = (share_slots < length).astype(jnp.float32)
    layer_out = ((resid_share + added) * live_share[:, None]).astype(jnp.bfloat16)
    live_rows = (slots < length)[:, None]
    key_rows = keys16.reshape(seq_len, k_cols)
    value_rows = values16.reshape(seq_len, k_cols)
    cache_rows = jnp.concatenate(
        [
            jnp.where(live_rows, key_rows, jnp.zeros_like(key_rows)),
            jnp.where(live_rows, value_rows, jnp.zeros_like(value_rows)),
        ],
        axis=1,
    )
    pages = cache_rows.reshape(seq_len // PAGE, PAGE, 2 * k_cols)
    pool_size = pages.shape[0]
    owner = lax.axis_index("req")
    targets = owner * pool_size + jnp.arange(pool_size, dtype=jnp.int32)
    picks = (page_slot[:, None] == targets[None, :]).astype(jnp.bfloat16)
    pool = jnp.einsum(
        "np,nsc->psc",
        picks,
        lax.all_gather(pages, "req", axis=0, tiled=True),
        preferred_element_type=jnp.float32,
    )
    kv_cache = pool.astype(jnp.bfloat16)
    return (layer_out, kv_cache)


def solution(mesh):
    return jax.shard_map(
        body,
        mesh=mesh,
        in_specs=(
            P("req", None),
            P("req"),
            P(),
            P(),
            P(("req", "tp"), None),
            P(("req", "tp"), None),
            P(),
            P(),
            P("tp", None),
            P("tp", None),
        ),
        out_specs=(P(("req", "tp"), None), P("req", None, "tp")),
        check_vma=False,
    )
```

profile of v0, /device:TPU:1, one launch (start us, length us, event | category | flops | bytes accessed | tf_op | source)
XLA Modules:
  0.0 472.2 jit_solution(814724774709201183)
XLA Ops:
  7.2 1.2 convert_element_type.60
  8.4 0.9 all_to_all.28
  9.3 1.0 copy.18
  10.3 10.0 %all_to_all.38 = bf16[20,4,960]{2,0,1:T(8,128)(2,1)S(1)} all-to-all(bf16[20,4,960]{2,0,1:T(8,128)(2,1)S(1)} %copy.18), channel_id=1, replica_groups=mesh['req'=32,'tp'=4] {'tp'}, dimensions={1} | all-to-all | bytes 307200 | tf_op jit(solution)/shard_map/all_to_all | solution.py:58
  22.4 1.0 scatter_custom_fusion
  23.4 2.3 fusion.4
  26.1 0.8 fusion.26
  27.0 43.9 %all-gather.4.cloned.1.call-done = bf16[2560,960]{1,0:T(8,128)(2,1)} async-done(((bf16[80,960]{1,0:T(8,128)(2,1)}), bf16[2560,960]{1,0:T(8,128)(2,1)}) %all-gather.4.cloned.1.call-update) | async-done | bytes 4915216 | tf_op jit(solution)/shard_map/all_gather | solution.py:73
  70.9 9.7 %reshape.159 = bf16[128,20,960]{2,1,0:T(8,128)(2,1)} reshape(bf16[2560,960]{1,0:T(8,128)(2,1)} %all-gather.4.cloned.1.call-done) | data formatting | bytes 9830400 | tf_op jit(solution)/shard_map/reshape | solution.py:76
  80.6 6.4 %gather_fusion = bf16[128,20,960]{2,1,0:T(8,128)(2,1)} fusion(bf16[128,20,960]{2,1,0:T(8,128)(2,1)} %reshape.159, s32[1024]{0:T(1024)S(1)} %pad_clamp_fusion), kind=kCustom, calls=%fused_computation | custom fusion | bytes 9830912 | tf_op jit(solution)/shard_map/gather | solution.py:76
  87.0 9.8 %reshape.160 = bf16[2560,960]{1,0:T(8,128)(2,1)} reshape(bf16[128,20,960]{2,1,0:T(8,128)(2,1)} %gather_fusion) | data formatting | bytes 9830400 | tf_op jit(solution)/shard_map/reshape | solution.py:76
  96.8 6.2 %fusion.13 = f32[512,960]{0,1:T(8,128)S(1)} fusion(bf16[2560,960]{1,0:T(8,128)(2,1)} %reshape.160, bf16[512,2560]{1,0:T(8,128)(2,1)} %param.10, f32[2560]{0:T(1024)S(1)} %copy-done.7, f32[512]{0:T(512)S(1)} %add_rsqrt_fusion.1), kind=kOutput, calls=%fused_computation.25 | convolution fusion | flops 2521825280 | bytes 9515008 | tf_op jit(solution)/shard_map/dot_general | solution.py:82
  103.9 1.0 subtract_convert_fusion
  105.6 7.6 %fusion.49 = (f32[2,4,512]{2,1,0:T(4,128)S(1)}, f32[2,4,512,512]{2,3,1,0:T(8,128)}) fusion(pred[512,512]{0,1:T(8,128)(4,1)} %fusion.26, bf16[512,2,4,40]{0,3,2,1:T(8,128)(2,1)} %bitcast.65, bf16[512,2,4,40]{0,3,2,1:T(8,128)(2,1)} %bitcast.64, bf16[512,2,40]{0,2,1:T(8,128)(2,1)} %get-tuple-element.15, bf16[512,2,40]{0,2,1:T(8,128)(2,1)S(1)} %get-tuple-element.14), kind=kOutput, calls=%fused_computation.76 | convolution fusion | flops 345571840 | bytes 9486336 | tf_op jit(solution)/shard_map/sub | solution.py:99
  113.2 4.2 fusion.22
  117.4 4.6 fusion.54
  122.1 2.4 convert_element_type.68
  124.5 1.3 all_to_all.32
  125.9 21.6 %all_to_all.39 = bf16[20,4,3456]{2,0,1:T(8,128)(2,1)} all-to-all(bf16[20,4,3456]{2,0,1:T(8,128)(2,1)S(1)} %copy.20), channel_id=1, replica_groups=mesh['req'=32,'tp'=4] {'tp'}, dimensions={1} | all-to-all | bytes 1105920 | tf_op jit(solution)/shard_map/all_to_all | solution.py:61
  147.5 2.0 all_to_all.35
  150.8 86.5 %all-reduce.2.cloned.1.call-done = f32[512,2560]{1,0:T(8,128)} async-done(((f32[512,2560]{1,0:T(8,128)}), f32[512,2560]{1,0:T(8,128)}) %all-reduce.2.cloned.1.call-update) | async-done | bytes 5242896 | tf_op jit(solution)/shard_map/psum | solution.py:108
  237.4 5.4 %multiply_reduce_fusion = (f32[512]{0:T(512)S(1)}, f32[512,2560]{1,0:T(8,128)}) fusion(f32[512,2560]{1,0:T(8,128)} %all-reduce.2.cloned.1.call-done, bf16[512,2560]{1,0:T(8,128)(2,1)S(1)} %copy-done.2), kind=kLoop, calls=%fused_computation.17 | loop fusion | flops 5242368 | bytes 13109248 | tf_op jit(solution)/shard_map/reduce_sum | solution.py:13
  242.8 72.6 %all-gather.6.cloned.1.call-done = bf16[2560,3456]{1,0:T(8,128)(2,1)} async-done(((bf16[80,3456]{1,0:T(8,128)(2,1)}), bf16[2560,3456]{1,0:T(8,128)(2,1)}) %all-gather.6.cloned.1.call-update) | async-done | bytes 17694736 | tf_op jit(solution)/shard_map/all_gather | solution.py:74
  315.4 24.5 %reshape.164 = bf16[128,20,3456]{2,1,0:T(8,128)(2,1)} reshape(bf16[2560,3456]{1,0:T(8,128)(2,1)} %all-gather.6.cloned.1.call-done) | data formatting | bytes 35389440 | tf_op jit(solution)/shard_map/reshape | solution.py:79
  339.9 17.0 %gather_fusion.1 = bf16[128,20,3456]{2,1,0:T(8,128)(2,1)} fusion(bf16[128,20,3456]{2,1,0:T(8,128)(2,1)} %reshape.164, s32[1024]{0:T(1024)S(1)} %pad_clamp_fusion), kind=kCustom, calls=%fused_computation.1 | custom fusion | bytes 35389952 | tf_op jit(solution)/shard_map/gather | solution.py:79
  356.9 25.1 %reshape.165 = bf16[2560,3456]{1,0:T(8,128)(2,1)} reshape(bf16[128,20,3456]{2,1,0:T(8,128)(2,1)} %gather_fusion.1) | data formatting | bytes 35389440 | tf_op jit(solution)/shard_map/reshape | solution.py:79
  382.0 15.3 %fusion.12 = f32[512,3456]{1,0:T(8,128)S(1)} fusion(bf16[2560,3456]{1,0:T(8,128)(2,1)} %reshape.165, f32[512,2560]{1,0:T(8,128)} %get-tuple-element.11, f32[2560]{0:T(1024)S(1)} %copy-done.8, f32[512]{0:T(512)S(1)} %add_rsqrt_fusion), kind=kOutput, calls=%fused_computation.24 | convolution fusion | flops 9063628800 | bytes 30027776 | tf_op jit(solution)/shard_map/dot_general | solution.py:112
  397.3 10.4 %fusion.19 = f32[512,2560]{1,0:T(8,128)} fusion(bf16[1728,2560]{1,0:T(8,128)(2,1)} %param.19, f32[512,3456]{1,0:T(8,128)S(1)} %fusion.12), kind=kOutput, calls=%fused_computation.30 | convolution fusion | flops 4535156736 | bytes 21430272 | tf_op jit(solution)/shard_map/dot_general | solution.py:114
  408.4 9.9 %fusion.23 = bf16[4,128,320]{1,0,2:T(4,128)(2,1)S(1)} fusion(bf16[128,128,320]{1,2,0:T(8,128)(2,1)} %all-gather.8.cloned.1.call-done, s32[128]{0:T(128)S(1)} %copy-done.6, s32[4]{0:T(128)S(1)} %iota_add_fusion), kind=kOutput, calls=%fused_computation.34 | convolution fusion | flops 42107392 | bytes 10813968 | tf_op jit(solution)/shard_map/np,nsc->psc/dot_general | solution.py:134
  418.3 0.8 copy.24
  419.1 43.9 %reduce-scatter.2.cloned.1.call-done = f32[128,2560]{1,0:T(8,128)} async-done(((f32[512,2560]{1,0:T(8,128)}), f32[128,2560]{1,0:T(8,128)}) %reduce-scatter.2.cloned.1.call-update) | async-done | bytes 1310736 | tf_op jit(solution)/shard_map/reduce_scatter | solution.py:115
  462.9 2.7 multiply_convert_fusion.2
  (52 shorter events, 5.4 us)
Async XLA Ops:
  7.2 110.3 %copy-start = (bf16[640,2560]{1,0:T(8,128)(2,1)S(1)}, bf16[640,2560]{1,0:T(8,128)(2,1)}, u32[]{:S(2)}) copy-start(bf16[640,2560]{1,0:T(8,128)(2,1)} %param.18) | copy-start | bytes 9830404
  7.2 63.7 %all-gather.4.cloned.1.call-start = ((), (), s32[]{:S(2)}) async-start(), calls=%async_computation.3 | async-start | bytes 5406720 | tf_op jit(solution)/shard_map/all_gather | solution.py:73
  21.0 216.3 %all-reduce.2.cloned.1.call-start = ((), (), s32[]{:S(2)}) async-start(), calls=%async_computation.4 | async-start | bytes 10485760 | tf_op jit(solution)/shard_map/psum | solution.py:108
  87.0 9.8 %copy-start.7 = (f32[2560]{0:T(1024)S(1)}, f32[2560]{0:T(1024)}, u32[]{:S(2)}) copy-start(f32[2560]{0:T(1024)} %param.16) | copy-start | bytes 30724
  105.6 7.6 %copy-start.5 = (bf16[512,160]{0,1:T(8,128)(2,1)S(1)}, bf16[512,160]{0,1:T(8,128)(2,1)}, u32[]{:S(2)}) copy-start(bf16[512,160]{0,1:T(8,128)(2,1)} %get-tuple-element.9) | copy-start | bytes 491524
  122.0 27.8 %copy-start.3 = (bf16[20,4,8,128]{3,2,1,0:T(8,128)(2,1)S(1)}, bf16[20,4,8,128]{3,2,1,0:T(8,128)(2,1)}, u32[]{:S(2)}) copy-start(bf16[20,4,8,128]{3,2,1,0:T(8,128)(2,1)} %get-tuple-element.8) | copy-start | bytes 491524
  122.0 27.8 %copy-start.4 = (bf16[512,2,40]{0,2,1:T(8,128)(2,1)S(1)}, bf16[512,2,40]{0,2,1:T(8,128)(2,1)}, u32[]{:S(2)}) copy-start(bf16[512,2,40]{0,2,1:T(8,128)(2,1)} %get-tuple-element.15) | copy-start | bytes 245764
  122.0 115.3 %copy-start.2 = (bf16[512,2560]{1,0:T(8,128)(2,1)S(1)}, bf16[512,2560]{1,0:T(8,128)(2,1)}, u32[]{:S(2)}) copy-start(bf16[512,2560]{1,0:T(8,128)(2,1)} %param.10) | copy-start | bytes 7864324
  122.1 193.3 %all-gather.6.cloned.1.call-start = ((), (), s32[]{:S(2)}) async-start(), calls=%async_computation.5 | async-start | bytes 18247680 | tf_op jit(solution)/shard_map/all_gather | solution.py:74
  149.6 258.2 %all-gather.8.cloned.1.call-start = ((), (), s32[]{:S(2)}) async-start(), calls=%async_computation.7 | async-start | bytes 10813440 | tf_op jit(solution)/shard_map/all_gather | solution.py:137
  150.8 312.2 %reduce-scatter.2.cloned.1.call-start = ((), (), s32[]{:S(2)}) async-start(), calls=%async_computation.6 | async-start | bytes 6553600 | tf_op jit(solution)/shard_map/reduce_scatter | solution.py:115
  356.9 25.1 %copy-start.8 = (f32[2560]{0:T(1024)S(1)}, f32[2560]{0:T(1024)}, u32[]{:S(2)}) copy-start(f32[2560]{0:T(1024)} %param.17) | copy-start | bytes 30724
  407.7 0.7 copy-start.6
  407.8 57.9 %copy-start.1 = (bf16[640,2560]{1,0:T(8,128)(2,1)S(1)}, bf16[640,2560]{1,0:T(8,128)(2,1)}, u32[]{:S(2)}) copy-start(bf16[640,2560]{1,0:T(8,128)(2,1)} %param.18) | copy-start | bytes 9830404
Sparse Core Ops, SparseCore 0:
  21.1 49.7 all-gather.3
  122.2 115.1 all-reduce.1
  240.3 75.0 all-gather.5
  318.1 57.3 all-gather.7
  407.9 55.0 reduce-scatter.1
where the time goes:
time: 474 us; the launch traced here: 472 us
  waiting for transfers between devices  247 us (52%)
  local copies, waits for them, and re-layouts  101 us (21%)
  matrix products  58.2 us (12%)
  blocking collectives  31.6 us (7%)
  other arithmetic  19.2 us (4%)
  between operations  14.6 us (3%)
    psum x1, waiting for transfers between devices, body(): mixed = lax.psum(partial_out, 'tp')  86.5 us
    all_gather x1, waiting for transfers between devices, body(): lax.all_gather(gu_half, 'req', axis=0, tiled=True)  72.6 us
    reshape x2, local copies, waits for them, and re-layouts, body(): gu_all.reshape(devices, rows_each, gu_all.shape[1])[inverse]  49.7 us
    all_gather x1, waiting for transfers between devices, body(): lax.all_gather(qkv_half, 'req', axis=0, tiled=True)  43.9 us
    reduce_scatter x1, waiting for transfers between devices, body(): added = lax.psum_scatter(down, 'tp', scatter_dimension=0, tiled=True)  43.9 us
    all_to_all x1, blocking collectives, body(): lax.all_to_all(trainer_gateup.astype(jnp.bfloat16), 'tp', split_axis=1, c...  21.6 us
    reshape x2, local copies, waits for them, and re-layouts, body(): qkv_all.reshape(devices, rows_each, qkv_all.shape[1])[inverse]  19.5 us
    gather x1, local copies, waits for them, and re-layouts, body(): gu_all.reshape(devices, rows_each, gu_all.shape[1])[inverse]  17 us
  transfers between devices with their start and end apart: 5, of which 4 were waited for; matrix products, arithmetic and copies ran while one was open for 25% of the time, Pallas kernels for 0%

commit v1 on v0

--- a/solution.py
+++ b/solution.py
@@ -70,7 +70,15 @@
         .set(jnp.arange(devices, dtype=jnp.int32))
     )
     qkv_all, gu_all = (
-        lax.all_gather(qkv_half, "req", axis=0, tiled=True),
+        jnp.concatenate(
+            jax.lax.all_to_all(
+                jnp.stack([qkv_half for _ in range(jax.lax.psum(1, "req"))]),
+                axis_name="req",
+                split_axis=0,
+                concat_axis=0,
+            ),
+            axis=0,
+        ),
         lax.all_gather(gu_half, "req", axis=0, tiled=True),
     )
     qkv_weight = qkv_all.reshape(devices, rows_each, qkv_all.shape[1])[inverse].reshape(

time: 474 us -> 431 us (0.909)
  waiting for transfers between devices: 247 us -> 190 us
  starting transfers between devices: 0.39 us -> 10.6 us
  local copies, waits for them, and re-layouts: 101 us -> 106 us
    all_gather x1, waiting for transfers between devices: 72.6 us -> 0.01 us  [body(): lax.all_gather(gu_half, 'req', axis=0, tiled=True)]
    all_to_all x0 -> x1, waiting for transfers between devices: none -> 56.2 us  [body(): jax.lax.all_to_all(jnp.stack([qkv_half for _ in range(jax.lax.psum(1, 're...]
    all_gather x1 -> x0, waiting for transfers between devices: 43.9 us -> none  [body(): lax.all_gather(qkv_half, 'req', axis=0, tiled=True)]
    another operation x0 -> x3, local copies, waits for them, and re-layouts: none -> 14.3 us  [the longest x1 9.72 us: body(): qkv_all.reshape(devices, rows_each, qkv_all.shape[1])[inverse]]
    all_to_all x0 -> x1, starting transfers between devices: none -> 10.2 us  [body(): jax.lax.all_to_all(jnp.stack([qkv_half for _ in range(jax.lax.psum(1, 're...]
    reshape x2 -> x1, local copies, waits for them, and re-layouts: 19.5 us -> 9.8 us  [body(): qkv_all.reshape(devices, rows_each, qkv_all.shape[1])[inverse]]
  transfers between devices with their start and end apart: 5 -> 5, of which waited for: 4 -> 3; matrix products, arithmetic and copies ran while one was open for 25% -> 27% of each run, Pallas kernels for 0% -> 0%
where the time goes in v1:
time: 431 us; the launch traced here: 428 us
  waiting for transfers between devices  190 us (44%)
  local copies, waits for them, and re-layouts  106 us (25%)
  matrix products  58.1 us (13%)
  blocking collectives  29.2 us (7%)
  other arithmetic  18.5 us (4%)
  between operations  16.4 us (4%)
  starting transfers between devices  10.6 us (2%)
    psum x1, waiting for transfers between devices, body(): mixed = lax.psum(partial_out, 'tp')  89.1 us
    all_to_all x1, waiting for transfers between devices, body(): jax.lax.all_to_all(jnp.stack([qkv_half for _ in range(jax.lax.psum(1, 're...  56.2 us
    reshape x2, local copies, waits for them, and re-layouts, body(): gu_all.reshape(devices, rows_each, gu_all.shape[1])[inverse]  49.7 us
    reduce_scatter x1, waiting for transfers between devices, body(): added = lax.psum_scatter(down, 'tp', scatter_dimension=0, tiled=True)  44.2 us
    all_to_all x1, blocking collectives, body(): lax.all_to_all(trainer_gateup.astype(jnp.bfloat16), 'tp', split_axis=1, c...  19.2 us
    gather x1, local copies, waits for them, and re-layouts, body(): gu_all.reshape(devices, rows_each, gu_all.shape[1])[inverse]  17.7 us
    dot_general x1, matrix products, body(): projected = jnp.dot(h_norm, gu_weight, preferred_element_type=jnp.float32)  15.3 us
    dot_general x1, matrix products, body(): down = jnp.dot(hidden, down_proj, preferred_element_type=jnp.float32)  10.4 us
  transfers between devices with their start and end apart: 5, of which 3 were waited for; matrix products, arithmetic and copies ran while one was open for 27% of the time, Pallas kernels for 0%

profile of v1, /device:TPU:1, one launch (start us, length us, event | category | flops | bytes accessed | tf_op | source)
XLA Modules:
  0.0 428.2 jit_solution(16896642384340402879)
XLA Ops:
  8.0 1.2 convert_element_type.60
  9.2 0.9 all_to_all.29
  10.1 1.0 copy.18
  11.1 10.0 %all_to_all.40 = bf16[20,4,960]{2,0,1:T(8,128)(2,1)S(1)} all-to-all(bf16[20,4,960]{2,0,1:T(8,128)(2,1)S(1)} %copy.18), channel_id=1, replica_groups=mesh['req'=32,'tp'=4] {'tp'}, dimensions={1} | all-to-all | bytes 307200 | tf_op jit(solution)/shard_map/all_to_all | solution.py:58
  21.8 3.9 stack.5
  25.7 10.2 %all-to-all-start.1 = ((bf16[32,80,960]{2,1,0:T(8,128)(2,1)}), bf16[32,80,960]{2,1,0:T(8,128)(2,1)}, u32[]{:S(2)}, u32[]{:S(2)}) async-start(bf16[32,80,960]{2,1,0:T(8,128)(2,1)} %stack.5), calls=%async_computation.1 | async-start | bytes 10485760 | tf_op jit(solution)/shard_map/all_to_all | solution.py:74
  36.6 1.0 scatter_custom_fusion
  37.6 2.3 fusion.4
  40.4 0.8 fusion.26
  41.2 56.2 %all-to-all-done.1 = bf16[32,80,960]{2,1,0:T(8,128)(2,1)} async-done(((bf16[32,80,960]{2,1,0:T(8,128)(2,1)}), bf16[32,80,960]{2,1,0:T(8,128)(2,1)}, u32[]{:S(2)}, u32[]{:S(2)}) %all-to-all-start.1) | async-done | bytes 4915232 | tf_op jit(solution)/shard_map/all_to_all | solution.py:74
  97.4 9.7 %reshape_reshape.3 = bf16[128,20,960]{2,1,0:T(8,128)(2,1)} reshape(bf16[32,80,960]{2,1,0:T(8,128)(2,1)} %all-to-all-done.1) | data formatting | bytes 9830400 | tf_op jit(solution)/shard_map/reshape;reshape | solution.py:84
  107.1 6.4 %gather_fusion = bf16[128,20,960]{2,1,0:T(8,128)(2,1)} fusion(bf16[128,20,960]{2,1,0:T(8,128)(2,1)} %reshape_reshape.3, s32[1024]{0:T(1024)S(1)} %pad_clamp_fusion), kind=kCustom, calls=%fused_computation | custom fusion | bytes 9830912 | tf_op jit(solution)/shard_map/gather | solution.py:84
  113.5 9.8 %reshape.159 = bf16[2560,960]{1,0:T(8,128)(2,1)} reshape(bf16[128,20,960]{2,1,0:T(8,128)(2,1)} %gather_fusion) | data formatting | bytes 9830400 | tf_op jit(solution)/shard_map/reshape | solution.py:84
  123.3 6.2 %fusion.13 = f32[512,960]{0,1:T(8,128)S(1)} fusion(bf16[2560,960]{1,0:T(8,128)(2,1)} %reshape.159, bf16[512,2560]{1,0:T(8,128)(2,1)} %param.10, f32[2560]{0:T(1024)S(1)} %copy-done.7, f32[512]{0:T(512)S(1)} %add_rsqrt_fusion.1), kind=kOutput, calls=%fused_computation.25 | convolution fusion | flops 2521825280 | bytes 9515008 | tf_op jit(solution)/shard_map/dot_general | solution.py:90
  130.3 1.0 subtract_convert_fusion
  132.1 7.6 %fusion.49 = (f32[2,4,512]{2,1,0:T(4,128)S(1)}, f32[2,4,512,512]{2,3,1,0:T(8,128)}) fusion(pred[512,512]{0,1:T(8,128)(4,1)} %fusion.26, bf16[512,2,4,40]{0,3,2,1:T(8,128)(2,1)} %bitcast.65, bf16[512,2,4,40]{0,3,2,1:T(8,128)(2,1)} %bitcast.64, bf16[512,2,40]{0,2,1:T(8,128)(2,1)} %get-tuple-element.15, bf16[512,2,40]{0,2,1:T(8,128)(2,1)S(1)} %get-tuple-element.14), kind=kOutput, calls=%fused_computation.76 | convolution fusion | flops 345571840 | bytes 9486336 | tf_op jit(solution)/shard_map/sub | solution.py:107
  139.6 4.2 fusion.22
  143.9 4.6 %fusion.54 = f32[512,2560]{1,0:T(8,128)} fusion(bf16[512,640]{0,1:T(8,128)(2,1)S(1)} %bitcast.62, bf16[640,2560]{1,0:T(8,128)(2,1)S(1)} %copy-done), kind=kOutput, calls=%fused_computation.77 | convolution fusion | flops 1677721600 | bytes 9175040 | tf_op jit(solution)/shard_map/dot_general | solution.py:111
  148.6 2.4 convert_element_type.68
  151.0 1.3 all_to_all.33
  152.4 19.2 %all_to_all.41 = bf16[20,4,3456]{2,0,1:T(8,128)(2,1)} all-to-all(bf16[20,4,3456]{2,0,1:T(8,128)(2,1)S(1)} %copy.20), channel_id=1, replica_groups=mesh['req'=32,'tp'=4] {'tp'}, dimensions={1} | all-to-all | bytes 1105920 | tf_op jit(solution)/shard_map/all_to_all | solution.py:61
  171.6 2.0 all_to_all.36
  174.8 89.1 %all-reduce.2.cloned.1.call-done = f32[512,2560]{1,0:T(8,128)} async-done(((f32[512,2560]{1,0:T(8,128)}), f32[512,2560]{1,0:T(8,128)}) %all-reduce.2.cloned.1.call-update) | async-done | bytes 5242896 | tf_op jit(solution)/shard_map/psum | solution.py:116
  264.0 5.4 %multiply_reduce_fusion = (f32[512]{0:T(512)S(1)}, f32[512,2560]{1,0:T(8,128)}) fusion(f32[512,2560]{1,0:T(8,128)} %all-reduce.2.cloned.1.call-done, bf16[512,2560]{1,0:T(8,128)(2,1)S(1)} %copy-done.2), kind=kLoop, calls=%fused_computation.17 | loop fusion | flops 5242368 | bytes 13109248 | tf_op jit(solution)/shard_map/reduce_sum | solution.py:13
  269.4 25.0 %reshape.163 = bf16[128,20,3456]{2,1,0:T(8,128)(2,1)} reshape(bf16[2560,3456]{1,0:T(8,128)(2,1)} %all-gather.3.cloned.1.call-done) | data formatting | bytes 35389440 | tf_op jit(solution)/shard_map/reshape | solution.py:87
  294.3 17.7 %gather_fusion.1 = bf16[128,20,3456]{2,1,0:T(8,128)(2,1)} fusion(bf16[128,20,3456]{2,1,0:T(8,128)(2,1)} %reshape.163, s32[1024]{0:T(1024)S(1)} %pad_clamp_fusion), kind=kCustom, calls=%fused_computation.1 | custom fusion | bytes 35389952 | tf_op jit(solution)/shard_map/gather | solution.py:87
  312.0 24.8 %reshape.164 = bf16[2560,3456]{1,0:T(8,128)(2,1)} reshape(bf16[128,20,3456]{2,1,0:T(8,128)(2,1)} %gather_fusion.1) | data formatting | bytes 35389440 | tf_op jit(solution)/shard_map/reshape | solution.py:87
  336.8 15.3 %fusion.12 = f32[512,3456]{1,0:T(8,128)S(1)} fusion(bf16[2560,3456]{1,0:T(8,128)(2,1)} %reshape.164, f32[512,2560]{1,0:T(8,128)} %get-tuple-element.11, f32[2560]{0:T(1024)S(1)} %copy-done.8, f32[512]{0:T(512)S(1)} %add_rsqrt_fusion), kind=kOutput, calls=%fused_computation.24 | convolution fusion | flops 9063628800 | bytes 30027776 | tf_op jit(solution)/shard_map/dot_general | solution.py:120
  352.1 10.4 %fusion.19 = f32[512,2560]{1,0:T(8,128)} fusion(bf16[1728,2560]{1,0:T(8,128)(2,1)} %param.19, f32[512,3456]{1,0:T(8,128)S(1)} %fusion.12), kind=kOutput, calls=%fused_computation.30 | convolution fusion | flops 4535156736 | bytes 21430272 | tf_op jit(solution)/shard_map/dot_general | solution.py:122
  363.2 9.9 %fusion.23 = bf16[4,128,320]{1,0,2:T(4,128)(2,1)S(1)} fusion(bf16[128,128,320]{1,2,0:T(8,128)(2,1)} %all-gather.5.cloned.1.call-done, s32[128]{0:T(128)S(1)} %copy-done.6, s32[4]{0:T(128)S(1)} %iota_add_fusion), kind=kOutput, calls=%fused_computation.34 | convolution fusion | flops 42107392 | bytes 10813968 | tf_op jit(solution)/shard_map/np,nsc->psc/dot_general | solution.py:142
  373.8 44.2 %reduce-scatter.2.cloned.1.call-done = f32[128,2560]{1,0:T(8,128)} async-done(((f32[512,2560]{1,0:T(8,128)}), f32[128,2560]{1,0:T(8,128)}) %reduce-scatter.2.cloned.1.call-update) | async-done | bytes 1310736 | tf_op jit(solution)/shard_map/reduce_scatter | solution.py:123
  418.1 2.7 multiply_convert_fusion.2
  (54 shorter events, 5.5 us)
Async XLA Ops:
  8.0 135.9 %copy-start = (bf16[640,2560]{1,0:T(8,128)(2,1)S(1)}, bf16[640,2560]{1,0:T(8,128)(2,1)}, u32[]{:S(2)}) copy-start(bf16[640,2560]{1,0:T(8,128)(2,1)} %param.18) | copy-start | bytes 9830404
  25.7 10.9 %copy-start.9 = (s32[128]{0:T(128)S(1)}, s32[128]{0:T(128)}, u32[]{:S(2)}) copy-start(s32[128]{0:T(128)} %param.13) | copy-start | bytes 1540
  25.7 71.7 %all-to-all-start.1 = ((bf16[32,80,960]{2,1,0:T(8,128)(2,1)}), bf16[32,80,960]{2,1,0:T(8,128)(2,1)}, u32[]{:S(2)}, u32[]{:S(2)}) async-start(bf16[32,80,960]{2,1,0:T(8,128)(2,1)} %stack.5), calls=%async_computation.1 | async-start | bytes 10485760 | tf_op jit(solution)/shard_map/all_to_all | solution.py:74
  35.9 228.1 %all-reduce.2.cloned.1.call-start = ((), (), s32[]{:S(2)}) async-start(), calls=%async_computation.4 | async-start | bytes 10485760 | tf_op jit(solution)/shard_map/psum | solution.py:116
  113.5 9.8 %copy-start.7 = (f32[2560]{0:T(1024)S(1)}, f32[2560]{0:T(1024)}, u32[]{:S(2)}) copy-start(f32[2560]{0:T(1024)} %param.16) | copy-start | bytes 30724
  132.1 7.6 %copy-start.5 = (bf16[512,160]{0,1:T(8,128)(2,1)S(1)}, bf16[512,160]{0,1:T(8,128)(2,1)}, u32[]{:S(2)}) copy-start(bf16[512,160]{0,1:T(8,128)(2,1)} %get-tuple-element.9) | copy-start | bytes 491524
  148.5 25.4 %copy-start.3 = (bf16[20,4,8,128]{3,2,1,0:T(8,128)(2,1)S(1)}, bf16[20,4,8,128]{3,2,1,0:T(8,128)(2,1)}, u32[]{:S(2)}) copy-start(bf16[20,4,8,128]{3,2,1,0:T(8,128)(2,1)} %get-tuple-element.8) | copy-start | bytes 491524
  148.5 25.4 %copy-start.4 = (bf16[512,2,40]{0,2,1:T(8,128)(2,1)S(1)}, bf16[512,2,40]{0,2,1:T(8,128)(2,1)}, u32[]{:S(2)}) copy-start(bf16[512,2,40]{0,2,1:T(8,128)(2,1)} %get-tuple-element.15) | copy-start | bytes 245764
  148.5 115.5 %copy-start.2 = (bf16[512,2560]{1,0:T(8,128)(2,1)S(1)}, bf16[512,2560]{1,0:T(8,128)(2,1)}, u32[]{:S(2)}) copy-start(bf16[512,2560]{1,0:T(8,128)(2,1)} %param.10) | copy-start | bytes 7864324
  148.5 120.9 %all-gather.3.cloned.1.call-start = ((), (), s32[]{:S(2)}) async-start(), calls=%async_computation.5 | async-start | bytes 18247680 | tf_op jit(solution)/shard_map/all_gather | solution.py:82
  173.6 189.0 %all-gather.5.cloned.1.call-start = ((), (), s32[]{:S(2)}) async-start(), calls=%async_computation.7 | async-start | bytes 10813440 | tf_op jit(solution)/shard_map/all_gather | solution.py:145
  174.8 243.3 %reduce-scatter.2.cloned.1.call-start = ((), (), s32[]{:S(2)}) async-start(), calls=%async_computation.6 | async-start | bytes 6553600 | tf_op jit(solution)/shard_map/reduce_scatter | solution.py:123
  312.0 24.8 %copy-start.8 = (f32[2560]{0:T(1024)S(1)}, f32[2560]{0:T(1024)}, u32[]{:S(2)}) copy-start(f32[2560]{0:T(1024)} %param.17) | copy-start | bytes 30724
  362.5 0.7 copy-start.6
  362.6 58.2 %copy-start.1 = (bf16[640,2560]{1,0:T(8,128)(2,1)S(1)}, bf16[640,2560]{1,0:T(8,128)(2,1)}, u32[]{:S(2)}) copy-start(bf16[640,2560]{1,0:T(8,128)(2,1)} %param.18) | copy-start | bytes 9830404
Sparse Core Ops, SparseCore 0:
  148.6 115.2 all-reduce.1
  362.7 55.3 reduce-scatter.1
Sparse Core Ops, SparseCore 1:
  173.7 76.5 all-gather.2
  252.9 57.2 all-gather.4
